TPU v7x, 512 devices: a whole 4x8x8 slice. The times are simulated.
512 devices in a mesh: row: 64 (over z, y), col: 8 (over x, core).
Axes of the slice: x: 4, y: 8, z: 8, core: 2. Of those that a mesh axis runs over, the one named last changes fastest.
Arguments:
- dinv0: bfloat16 [65536, 4096], P('row', 'col'), as said below
- dinv1: bfloat16 [32768, 4096], P('row', 'col'), as said below
- dinv2: bfloat16 [16384, 4096], P('row', 'col'), as said below
- offdiag0: bfloat16 [65536, 4096], P('row', 'col'), may hold values from -0.0625 to 0.0625
- offdiag1: bfloat16 [32768, 4096], P('row', 'col'), may hold values from -0.0625 to 0.0625
- rhs0: bfloat16 [65536, 128], P(('row', 'col')), may hold values from -6 to 6
- rhs1: bfloat16 [32768, 128], P(('row', 'col')), may hold values from -6 to 6
- rhs2: bfloat16 [16384, 128], P(('row', 'col')), may hold values from -6 to 6
- block_rows0: int32 [16, 64, 16], replicated, may hold values from 0 to 63, all different within a row
- block_rows1: int32 [8, 64, 16], replicated, may hold values from 0 to 63, all different within a row
Outputs:
- solution0: float32 [65536, 128], P(('row', 'col'))
- solution1: float32 [32768, 128], P(('row', 'col'))
- solution2: float32 [16384, 128], P(('row', 'col'))
Inputs may be any that keep to these rules, and one draw needn't show every extreme that they name: `block_rows0`: each row of the last dimension lists 16 different block rows. `block_rows1`: each row of the last dimension lists 16 different block rows. `dinv0`: each supernode's block is lower triangular in global order, with a positive diagonal. `dinv1`: each supernode's block is lower triangular in global order, with a positive diagonal. `dinv2`: each supernode's block is lower triangular in global order, with a positive diagonal.
All inputs are finite; a program needn't handle non-finite values.
Results may differ from a plain program's by a relative error of at most 0.0095.
Values may be sent and summed in bfloat16 or wider, within the bound.
No kernel may reach another device: no remote copies, remote signals or barrier semaphores. Data moves between devices by JAX's collectives and lax.ppermute only.
A program may use at most 64 MiB of HBM per device.

v0:
```python
import jax
import jax.numpy as jnp
from jax import lax
from jax.experimental import pallas as pl
from jax.experimental.pallas import tpu as pltpu
from jax.sharding import PartitionSpec as P


MB = 64
GR = 4
CORES = 2


def row_groups(row_devs, group):
    return [[first + r for r in range(group)] for first in range(0, row_devs, group)]


def family_groups(row_devs, col_devs, group):
    return [
        [(first + s * group + r) * col_devs + c for s in range(2) for c in range(col_devs)]
        for first in range(0, row_devs, 2 * group)
        for r in range(group)
    ]


def chip_groups(col_devs):
    return [[core + CORES * chip for chip in range(col_devs // CORES)] for core in range(CORES)]


def swap(values):
    middle = values.shape[-1] // 2
    return jnp.concatenate((values[..., middle:], values[..., :middle]), axis=-1)


def exchange(slots, axis, groups=None):
    return lax.all_to_all(slots, axis, 0, 0, axis_index_groups=groups, tiled=True)


def share(piece, count, axis, groups=None):
    slots = lax.optimization_barrier(jnp.broadcast_to(piece[None], (count,) + piece.shape))
    return exchange(slots, axis, groups)


def kept(values, listings, group):
    row_blocks = values.shape[0] // MB
    position = lax.axis_index("row")
    owned = jnp.arange(row_blocks, dtype=jnp.int32) * group + position % group
    listing = lax.dynamic_index_in_dim(listings, position // group, 0, keepdims=False)
    listed = jnp.any(listing[None, :, :] == owned[:, None, None], axis=-1)
    blocks = listed.shape[1]
    columns = lax.broadcasted_iota(jnp.int32, (blocks, values.shape[1]), 1) // (values.shape[1] // blocks)
    spread = (columns == lax.broadcasted_iota(jnp.int32, columns.shape, 0)).astype(jnp.bfloat16)
    return jnp.dot(listed.astype(jnp.bfloat16), spread, preferred_element_type=jnp.float32) > 0.5


def coupling(values, keeping):
    shaped = values.reshape(keeping.shape[0], MB, -1)
    return jnp.where(keeping[:, None, :], shaped, jnp.zeros_like(shaped)).reshape(values.shape)


def duplicate(source_ref, target_ref, held_ref, in_sems, out_sems):
    steps, rows = held_ref.shape[:2]
    loads = [
        pltpu.make_async_copy(source_ref.at[pl.ds(i * rows, rows)], held_ref.at[i], in_sems.at[i])
        for i in range(steps)
    ]
    stores = [
        pltpu.make_async_copy(held_ref.at[i], target_ref.at[pl.ds(i * rows, rows)], out_sems.at[i])
        for i in range(steps)
    ]
    for load in loads:
        load.start()
    for load, store in zip(loads, stores):
        load.wait()
        store.start()
    for store in stores:
        store.wait()


def second_copy(values, steps=4):
    rows, columns = values.shape
    return pl.pallas_call(
        duplicate,
        in_specs=[pl.BlockSpec(memory_space=pl.ANY)],
        out_specs=pl.BlockSpec(memory_space=pl.ANY),
        out_shape=jax.ShapeDtypeStruct(values.shape, values.dtype),
        scratch_shapes=[
            pltpu.VMEM((steps, rows // steps, columns), values.dtype),
            pltpu.SemaphoreType.DMA((steps,)),
            pltpu.SemaphoreType.DMA((steps,)),
        ],
    )(values)


def per_device(dinv0, dinv1, dinv2, offdiag0, offdiag1, rhs0, rhs1, rhs2, block_rows0, block_rows1):
    row_devs = lax.axis_size("row")
    col_devs = lax.axis_size("col")
    unit = MB // col_devs
    width = rhs0.shape[1]
    groups = (GR, 2 * GR, 4 * GR)
    own = [row_groups(row_devs, group) for group in groups]
    family = family_groups(row_devs, col_devs, groups[1])
    half = lax.axis_index("row") // groups[0] % 2
    upper = lax.axis_index("row") // groups[1] % 2
    column = lax.axis_index("col")
    chips = col_devs // CORES
    lanes = lax.broadcasted_iota(jnp.int32, (1, width), 1) // (width // CORES)
    low = lanes == 0

    def plain(matrix, vector):
        return jnp.dot(matrix, vector, preferred_element_type=jnp.float32)

    def transposed(matrix, vector):
        return jnp.einsum("ij,in->jn", matrix, vector, preferred_element_type=jnp.float32)

    def apply_plain(matrix, vector):
        return plain(matrix, vector).astype(jnp.bfloat16)

    def apply_transposed(matrix, vector):
        return transposed(matrix, vector).astype(jnp.bfloat16)

    def total(slots):
        return jnp.sum(slots.astype(jnp.float32), axis=0)

    def row_gather(piece, level):
        return share(piece, groups[level], "row", own[level])

    def flat(gathered):
        return gathered.transpose(1, 0, 2, 3).reshape(-1, width)

    def column_slots(product):
        return product.reshape(-1, col_devs, unit, width).transpose(1, 0, 2, 3)

    def column_sum(product):
        return total(exchange(column_slots(product), "col"))

    def row_sum(product, level):
        slots = product.reshape(-1, groups[level], unit, width).transpose(1, 0, 2, 3)
        return total(exchange(slots, "row", own[level]))

    gathered, kept0, kept1, inverse0, other2 = lax.optimization_barrier(
        (
            row_gather(rhs0.reshape(-1, unit, width), 0),
            kept(offdiag0, block_rows0, groups[0]),
            kept(offdiag1, block_rows1, groups[1]),
            dinv0,
            lax.ppermute(dinv2, "col", [(i, i ^ 1) for i in range(col_devs)]),
        )
    )
    slots, late1, late2, half, upper, column = lax.optimization_barrier(
        (column_slots(apply_plain(inverse0, flat(gathered))), rhs1, rhs2, half, upper, column)
    )
    received = exchange(slots, "col")
    again0 = second_copy(inverse0)
    mine = lax.broadcasted_iota(jnp.int32, (1, 2, 1, 1), 1) == half
    destination = lax.broadcasted_iota(jnp.int32, (1, 2 * col_devs, 1, 1), 1)
    here = destination == upper * col_devs + column
    received, again0, side1, side2, first, near, low, spot = lax.optimization_barrier(
        (
            received,
            again0,
            jnp.where(mine, late1.reshape(-1, 1, unit, width).astype(jnp.float32), 0.0),
            jnp.where(here, late2.reshape(-1, 1, unit, width).astype(jnp.float32), 0.0),
            half == 0,
            lanes == column % CORES,
            low,
            upper * col_devs + column,
        )
    )
    solved0 = total(received).astype(jnp.bfloat16)
    gathered, kept0 = lax.optimization_barrier((row_gather(solved0, 0), kept0))
    update = column_sum(apply_plain(coupling(offdiag0, kept0), flat(gathered)))
    update = update.reshape(-1, 2, unit, width)
    gathered = row_gather((side1 - update).astype(jnp.bfloat16), 1)
    gathered = gathered.reshape(2, groups[0], -1, unit, width)
    residual = total(gathered).astype(jnp.bfloat16)

    solved1 = column_sum(apply_plain(dinv1, flat(residual))).astype(jnp.bfloat16)
    gathered, kept1 = lax.optimization_barrier((row_gather(solved1, 1), kept1))
    partial_value = plain(coupling(offdiag1, kept1), flat(gathered)).reshape(-1, 2 * col_devs, unit, width)
    partial_value = (side2 - partial_value).astype(jnp.bfloat16)
    even, odd = (
        partial_value.reshape(-1, 2, chips, CORES, unit, width)[:, :, :, u].transpose(1, 2, 0, 3, 4)
        for u in range(CORES)
    )
    slots = jnp.stack((jnp.where(low, even, swap(odd)), jnp.where(low, swap(even), odd)), axis=2)
    slots = slots.reshape(2 * col_devs, -1, unit, width)
    residual = total(exchange(slots, ("row", "col"), family)).astype(jnp.bfloat16)

    vector = flat(row_gather(residual, 2))
    turned = swap(vector)
    product = plain(dinv2, jnp.where(near, vector, turned)) + plain(other2, jnp.where(near, turned, vector))
    product = product.astype(jnp.bfloat16)
    tall = product.shape[0] // CORES
    shared = share(jnp.where(low, product[:tall], product[tall:]), chips, "col", chip_groups(col_devs))
    packed = total(shared).astype(jnp.bfloat16)
    turned = swap(packed)
    row_form = jnp.concatenate((jnp.where(low, packed, turned), jnp.where(low, turned, packed)), axis=0)
    product = jnp.where(near, transposed(dinv2, row_form), transposed(other2, row_form))
    pieces2 = row_sum(product.astype(jnp.bfloat16), 2)

    gathered = share(pieces2.astype(jnp.bfloat16), 2 * col_devs, ("row", "col"), family)
    even, odd = (gathered.reshape(2, chips, CORES, -1, unit, width)[:, :, k] for k in range(CORES))
    gathered = jnp.stack((jnp.where(low, even, swap(odd)), jnp.where(low, swap(even), odd)), axis=3)
    gathered = gathered.transpose(2, 0, 1, 3, 4, 5)
    gathered, pieces2 = lax.optimization_barrier((gathered, pieces2))
    own_unit = lax.dynamic_slice_in_dim(
        gathered.reshape(-1, 2 * col_devs, unit, width), spot, 1, 1, allow_negative_indices=False
    )
    own_unit = own_unit.reshape(pieces2.shape).astype(jnp.float32)
    answer2 = jnp.where(near, pieces2, own_unit)
    gathered, kept1, answer2 = lax.optimization_barrier((gathered, kept1, answer2))
    carried = row_sum(apply_transposed(coupling(offdiag1, kept1), gathered.reshape(-1, width)), 1)
    weighted = (solved1.astype(jnp.float32) - carried).astype(jnp.bfloat16)
    product = apply_transposed(dinv1, flat(share(weighted, col_devs, "col")))
    slots = product.reshape(-1, 2, groups[0], unit, width).transpose(2, 0, 1, 3, 4)
    slots = jnp.broadcast_to(slots[None], (2,) + slots.shape).reshape(groups[1], -1, unit, width)
    both = total(exchange(slots, "row", own[1]))
    pairs = both.reshape(-1, 2, unit, width)
    answer1 = jnp.where(first, pairs[:, 0], pairs[:, 1])
    both, answer1 = lax.optimization_barrier((both, answer1))

    gathered, kept0 = lax.optimization_barrier((share(both.astype(jnp.bfloat16), col_devs, "col"), kept0))
    carried = row_sum(apply_transposed(coupling(offdiag0, kept0), flat(gathered)), 0)
    weighted = (solved0.astype(jnp.float32) - carried).astype(jnp.bfloat16)
    answer0 = row_sum(apply_transposed(again0, flat(share(weighted, col_devs, "col"))), 0)
    return tuple(answer.reshape(-1, width) for answer in (answer0, answer1, answer2))


def solution(mesh):
    placed = (
        P("row", "col"),
        P("row", "col"),
        P("row", "col"),
        P("row", "col"),
        P("row", "col"),
        P(("row", "col"), None),
        P(("row", "col"), None),
        P(("row", "col"), None),
        P(),
        P(),
    )
    return jax.shard_map(
        per_device,
        mesh=mesh,
        in_specs=placed,
        out_specs=(P(("row", "col"), None), P(("row", "col"), None), P(("row", "col"), None)),
        check_vma=False,
    )
```

profile of v0, /device:TPU:128, one launch (start us, length us, event | category | flops | bytes accessed | tf_op | source)
XLA Modules:
  0.0 217.2 jit_solution(16872826954041613202)
XLA Ops:
  0.7 1.5 broadcast_in_dim.210
  2.2 4.9 %all-to-all-start = ((bf16[4,16,8,128]{3,2,1,0:T(8,128)(2,1)}), bf16[4,16,8,128]{3,2,1,0:T(8,128)(2,1)S(1)}, u32[]{:S(2)}, u32[]{:S(2)}) async-start(bf16[4,16,8,128]{3,2,1,0:T(8,128)(2,1)} %broadcast_in_dim.210), calls=%async_computation | async-start | bytes 262144 | tf_op jit(solution)/shard_map/all_to_all | solution.py:36
  7.1 1.9 collective-permute-start
  11.1 2.1 all-to-all-done
  14.4 2.0 shard_map.121
  16.5 4.4 %all-to-all-start.1 = ((bf16[8,16,8,128]{3,2,1,0:T(8,128)(2,1)}), bf16[8,16,8,128]{3,2,1,0:T(8,128)(2,1)S(1)}, u32[]{:S(2)}, u32[]{:S(2)}) async-start(bf16[8,16,8,128]{3,2,1,0:T(8,128)(2,1)} %bitcast.160), calls=%async_computation.1 | async-start | bytes 524288 | tf_op jit(solution)/shard_map/all_to_all | solution.py:36
  21.1 7.3 %all-to-all-done.1 = bf16[8,16,8,128]{3,2,1,0:T(8,128)(2,1)S(1)} async-done(((bf16[8,16,8,128]{3,2,1,0:T(8,128)(2,1)}), bf16[8,16,8,128]{3,2,1,0:T(8,128)(2,1)S(1)}, u32[]{:S(2)}, u32[]{:S(2)}) %all-to-all-start.1) | async-done | bytes 262176 | tf_op jit(solution)/shard_map/all_to_all | solution.py:36
  28.5 8.9 %all_to_all.95 = bf16[4,16,8,128]{3,2,1,0:T(8,128)(2,1)S(1)} all-to-all(bf16[4,16,8,128]{3,2,1,0:T(8,128)(2,1)S(1)} %broadcast_in_dim.217), channel_id=1, replica_groups={{0,8,16,24},{32,40,48,56},{64,72,80,88},{96,104,112,120},{128,136,144,1..., dimensions={0} | all-to-all | bytes 262144 | tf_op jit(solution)/shard_map/all_to_all | solution.py:36
  38.0 9.9 %all_to_all.96 = bf16[8,16,8,128]{3,2,1,0:T(8,128)(2,1)S(1)} all-to-all(bf16[8,16,8,128]{3,2,1,0:T(8,128)(2,1)S(1)} %bitcast.169), channel_id=1, replica_groups=mesh['row'=64,'col'=8] {'col'}, dimensions={0} | all-to-all | bytes 524288 | tf_op jit(solution)/shard_map/all_to_all | solution.py:36
  48.0 16.8 %all_to_all.97 = bf16[8,8,2,8,128]{4,3,2,1,0:T(8,128)(2,1)S(1)} all-to-all(bf16[8,8,2,8,128]{4,3,2,1,0:T(8,128)(2,1)S(1)} %broadcast_in_dim.220), channel_id=1, replica_groups={{0,8,16,24,32,40,48,56},{64,72,80,88,96,104,112,120},{128,136,144,152,1..., dimensions={0} | all-to-all | bytes 524288 | tf_op jit(solution)/shard_map/all_to_all | solution.py:36
  65.4 8.6 %all_to_all.98 = bf16[8,8,8,128]{3,2,1,0:T(8,128)(2,1)S(1)} all-to-all(bf16[8,8,8,128]{3,2,1,0:T(8,128)(2,1)S(1)} %copy.129), channel_id=1, replica_groups=mesh['row'=64,'col'=8] {'col'}, dimensions={0} | all-to-all | bytes 262144 | tf_op jit(solution)/shard_map/all_to_all | solution.py:36
  74.1 11.5 %all_to_all.99 = bf16[8,8,8,128]{3,2,1,0:T(8,128)(2,1)S(1)} all-to-all(bf16[8,8,8,128]{3,2,1,0:T(8,128)(2,1)S(1)} %broadcast_in_dim.226), channel_id=1, replica_groups={{0,8,16,24,32,40,48,56},{64,72,80,88,96,104,112,120},{128,136,144,152,1..., dimensions={0} | all-to-all | bytes 262144 | tf_op jit(solution)/shard_map/all_to_all | solution.py:36
  86.4 10.8 %all_to_all.100 = bf16[16,4,8,128]{3,2,1,0:T(8,128)(2,1)S(1)} all-to-all(bf16[16,4,8,128]{3,2,1,0:T(8,128)(2,1)S(1)} %bitcast.179), channel_id=1, replica_groups={{0,1,2,3,4,5,6,7,64,65,66,67,68,69,70,71},{8,9,10,11,12,13,14,15,72,73,..., dimensions={0} | all-to-all | bytes 262144 | tf_op jit(solution)/shard_map/all_to_all | solution.py:36
  97.3 11.5 %all_to_all.101 = bf16[16,4,8,128]{3,2,1,0:T(8,128)(2,1)S(1)} all-to-all(bf16[16,4,8,128]{3,2,1,0:T(8,128)(2,1)S(1)} %broadcast_in_dim.229), channel_id=1, replica_groups={{0,8,16,24,32,40,48,56,64,72,80,88,96,104,112,120},{128,136,144,152,160..., dimensions={0} | all-to-all | bytes 262144 | tf_op jit(solution)/shard_map/all_to_all | solution.py:36
  110.5 8.4 %all_to_all.102 = bf16[4,128,128]{2,1,0:T(8,128)(2,1)S(1)} all-to-all(bf16[4,128,128]{2,1,0:T(8,128)(2,1)S(1)} %broadcast_in_dim.230), channel_id=1, replica_groups={{0,2,4,6},{1,3,5,7},{8,10,12,14},{9,11,13,15},{16,18,20,22},{17,19,21,2..., dimensions={0} | all-to-all | bytes 262144 | tf_op jit(solution)/shard_map/all_to_all | solution.py:36
  119.7 11.7 %all_to_all.103 = bf16[16,4,8,128]{3,2,1,0:T(8,128)(2,1)S(1)} all-to-all(bf16[16,4,8,128]{3,2,1,0:T(8,128)(2,1)S(1)} %copy.147), channel_id=1, replica_groups={{0,8,16,24,32,40,48,56,64,72,80,88,96,104,112,120},{128,136,144,152,160..., dimensions={0} | all-to-all | bytes 262144 | tf_op jit(solution)/shard_map/all_to_all | solution.py:36
  131.4 9.4 %all_to_all.104 = bf16[16,4,8,128]{3,2,1,0:T(8,128)(2,1)S(1)} all-to-all(bf16[16,4,8,128]{3,2,1,0:T(8,128)(2,1)S(1)} %broadcast_in_dim.231), channel_id=1, replica_groups={{0,1,2,3,4,5,6,7,64,65,66,67,68,69,70,71},{8,9,10,11,12,13,14,15,72,73,..., dimensions={0} | all-to-all | bytes 262144 | tf_op jit(solution)/shard_map/all_to_all | solution.py:36
  142.3 11.8 %all_to_all.105 = bf16[8,8,8,128]{3,2,1,0:T(8,128)(2,1)S(1)} all-to-all(bf16[8,8,8,128]{3,2,1,0:T(8,128)(2,1)S(1)} %bitcast.184), channel_id=1, replica_groups={{0,8,16,24,32,40,48,56},{64,72,80,88,96,104,112,120},{128,136,144,152,1..., dimensions={0} | all-to-all | bytes 262144 | tf_op jit(solution)/shard_map/all_to_all | solution.py:36
  154.2 8.5 %all_to_all.106 = bf16[8,8,8,128]{3,2,1,0:T(8,128)(2,1)S(1)} all-to-all(bf16[8,8,8,128]{3,2,1,0:T(8,128)(2,1)S(1)} %broadcast_in_dim.235), channel_id=1, replica_groups=mesh['row'=64,'col'=8] {'col'}, dimensions={0} | all-to-all | bytes 262144 | tf_op jit(solution)/shard_map/all_to_all | solution.py:36
  163.1 14.4 %all_to_all.107 = bf16[8,16,8,128]{3,2,1,0:T(8,128)(2,1)S(1)} all-to-all(bf16[8,16,8,128]{3,2,1,0:T(8,128)(2,1)S(1)} %bitcast.171), channel_id=1, replica_groups={{0,8,16,24,32,40,48,56},{64,72,80,88,96,104,112,120},{128,136,144,152,1..., dimensions={0} | all-to-all | bytes 524288 | tf_op jit(solution)/shard_map/all_to_all | solution.py:36
  178.2 9.9 %all_to_all.108 = bf16[8,16,8,128]{3,2,1,0:T(8,128)(2,1)S(1)} all-to-all(bf16[8,16,8,128]{3,2,1,0:T(8,128)(2,1)S(1)} %broadcast_in_dim.237), channel_id=1, replica_groups=mesh['row'=64,'col'=8] {'col'}, dimensions={0} | all-to-all | bytes 524288 | tf_op jit(solution)/shard_map/all_to_all | solution.py:36
  188.8 8.6 %all_to_all.109 = bf16[4,16,8,128]{3,2,1,0:T(8,128)(2,1)S(1)} all-to-all(bf16[4,16,8,128]{3,2,1,0:T(8,128)(2,1)S(1)} %bitcast.186), channel_id=1, replica_groups={{0,8,16,24},{32,40,48,56},{64,72,80,88},{96,104,112,120},{128,136,144,1..., dimensions={0} | all-to-all | bytes 262144 | tf_op jit(solution)/shard_map/all_to_all | solution.py:36
  197.5 9.9 %all_to_all.110 = bf16[8,16,8,128]{3,2,1,0:T(8,128)(2,1)S(1)} all-to-all(bf16[8,16,8,128]{3,2,1,0:T(8,128)(2,1)S(1)} %broadcast_in_dim.240), channel_id=1, replica_groups=mesh['row'=64,'col'=8] {'col'}, dimensions={0} | all-to-all | bytes 524288 | tf_op jit(solution)/shard_map/all_to_all | solution.py:36
  208.0 8.5 %all_to_all.111 = bf16[4,16,8,128]{3,2,1,0:T(8,128)(2,1)S(1)} all-to-all(bf16[4,16,8,128]{3,2,1,0:T(8,128)(2,1)S(1)} %bitcast.187), channel_id=1, replica_groups={{0,8,16,24},{32,40,48,56},{64,72,80,88},{96,104,112,120},{128,136,144,1..., dimensions={0} | all-to-all | bytes 262144 | tf_op jit(solution)/shard_map/all_to_all | solution.py:36
  (119 shorter events, 12.5 us)
Async XLA Ops:
  0.6 64.3 %copy-start = (bf16[512,512]{1,0:T(8,128)(2,1)S(1)}, bf16[512,512]{1,0:T(8,128)(2,1)}, u32[]{:S(2)}) copy-start(bf16[512,512]{1,0:T(8,128)(2,1)} %param.11) | copy-start | bytes 1572868
  0.6 12.5 %copy-start.1 = (bf16[1024,512]{1,0:T(8,128)(2,1)S(1)}, bf16[1024,512]{1,0:T(8,128)(2,1)}, u32[]{:S(2)}) copy-start(bf16[1024,512]{1,0:T(8,128)(2,1)} %source_ref) | copy-start | bytes 3145732
  2.2 10.9 %all-to-all-start = ((bf16[4,16,8,128]{3,2,1,0:T(8,128)(2,1)}), bf16[4,16,8,128]{3,2,1,0:T(8,128)(2,1)S(1)}, u32[]{:S(2)}, u32[]{:S(2)}) async-start(bf16[4,16,8,128]{3,2,1,0:T(8,128)(2,1)} %broadcast_in_dim.210), calls=%async_computation | async-start | bytes 262144 | tf_op jit(solution)/shard_map/all_to_all | solution.py:36
  7.1 6.1 %collective-permute-start = (bf16[256,512]{1,0:T(8,128)(2,1)}, bf16[256,512]{1,0:T(8,128)(2,1)S(1)}, u32[]{:S(2)}, u32[]{:S(2)}) collective-permute-start(bf16[256,512]{1,0:T(8,128)(2,1)} %param.12), channel_id=1, source_target_pairs={{0,1},{1,0},{2,3},{3,2},{4,5},{5,4},{6,7},{7,6},{8,9},{9,8},{10,11... | collective-permute-start | bytes 786440 | tf_op jit(solution)/shard_map/ppermute | solution.py:147
  14.4 6.6 %copy-start.7 = (bf16[32,128]{1,0:T(8,128)(2,1)S(1)}, bf16[32,128]{1,0:T(8,128)(2,1)}, u32[]{:S(2)}) copy-start(bf16[32,128]{1,0:T(8,128)(2,1)} %param.17) | copy-start | bytes 24580
  14.4 6.6 %copy-start.6 = (bf16[64,128]{1,0:T(8,128)(2,1)S(1)}, bf16[64,128]{1,0:T(8,128)(2,1)}, u32[]{:S(2)}) copy-start(bf16[64,128]{1,0:T(8,128)(2,1)} %param.16) | copy-start | bytes 49156
  16.4 21.0 %copy-start.2 = (bf16[1024,512]{1,0:T(8,128)(2,1)S(1)}, bf16[1024,512]{1,0:T(8,128)(2,1)}, u32[]{:S(2)}) copy-start(bf16[1024,512]{1,0:T(8,128)(2,1)} %param.13) | copy-start | bytes 3145732
  16.5 11.9 %all-to-all-start.1 = ((bf16[8,16,8,128]{3,2,1,0:T(8,128)(2,1)}), bf16[8,16,8,128]{3,2,1,0:T(8,128)(2,1)S(1)}, u32[]{:S(2)}, u32[]{:S(2)}) async-start(bf16[8,16,8,128]{3,2,1,0:T(8,128)(2,1)} %bitcast.160), calls=%async_computation.1 | async-start | bytes 524288 | tf_op jit(solution)/shard_map/all_to_all | solution.py:36
  65.4 20.3 %copy-start.4 = (bf16[512,512]{1,0:T(8,128)(2,1)S(1)}, bf16[512,512]{1,0:T(8,128)(2,1)}, u32[]{:S(2)}) copy-start(bf16[512,512]{1,0:T(8,128)(2,1)} %param.14) | copy-start | bytes 1572868
  108.8 1.0 copy-start.5
  188.8 18.7 %copy-start.3 = (bf16[1024,512]{1,0:T(8,128)(2,1)S(1)}, bf16[1024,512]{1,0:T(8,128)(2,1)}, u32[]{:S(2)}) copy-start(bf16[1024,512]{1,0:T(8,128)(2,1)} %shard_map.121) | copy-start | bytes 3145732
where the time goes:
time: 218 us; the launch traced here: 217 us
  blocking collectives  179 us (82%)
  starting transfers between devices  11.2 us (5%)
  waiting for transfers between devices  9.37 us (4%)
  local copies, waits for them, and re-layouts  6.44 us (3%)
  matrix products  4.17 us (2%)
  other arithmetic  3.38 us (2%)
    all_to_all x17, blocking collectives, exchange(): lax.all_to_all(slots, axis, 0, 0, axis_index_groups=groups, tiled=True)  179 us
    all_to_all x2, waiting for transfers between devices, exchange(): lax.all_to_all(slots, axis, 0, 0, axis_index_groups=groups, tiled=True)  9.36 us
    all_to_all x2, starting transfers between devices, exchange(): lax.all_to_all(slots, axis, 0, 0, axis_index_groups=groups, tiled=True)  9.31 us
  transfers between devices with their start and end apart: 3, of which 2 were waited for; matrix products, arithmetic and copies ran while one was open for 1% of the time, Pallas kernels for 0%

commit v1 on v0

--- a/solution.py
+++ b/solution.py
@@ -138,12 +138,13 @@
         slots = product.reshape(-1, groups[level], unit, width).transpose(1, 0, 2, 3)
         return total(exchange(slots, "row", own[level]))
 
-    gathered, kept0, kept1, inverse0, other2 = lax.optimization_barrier(
+    gathered, kept0, kept1, inverse0, inverse2, other2 = lax.optimization_barrier(
         (
             row_gather(rhs0.reshape(-1, unit, width), 0),
             kept(offdiag0, block_rows0, groups[0]),
             kept(offdiag1, block_rows1, groups[1]),
             dinv0,
+            dinv2,
             lax.ppermute(dinv2, "col", [(i, i ^ 1) for i in range(col_devs)]),
         )
     )
@@ -189,14 +190,14 @@
 
     vector = flat(row_gather(residual, 2))
     turned = swap(vector)
-    product = plain(dinv2, jnp.where(near, vector, turned)) + plain(other2, jnp.where(near, turned, vector))
+    product = plain(inverse2, jnp.where(near, vector, turned)) + plain(other2, jnp.where(near, turned, vector))
     product = product.astype(jnp.bfloat16)
     tall = product.shape[0] // CORES
     shared = share(jnp.where(low, product[:tall], product[tall:]), chips, "col", chip_groups(col_devs))
     packed = total(shared).astype(jnp.bfloat16)
     turned = swap(packed)
     row_form = jnp.concatenate((jnp.where(low, packed, turned), jnp.where(low, turned, packed)), axis=0)
-    product = jnp.where(near, transposed(dinv2, row_form), transposed(other2, row_form))
+    product = jnp.where(near, transposed(inverse2, row_form), transposed(other2, row_form))
     pieces2 = row_sum(product.astype(jnp.bfloat16), 2)
 
     gathered = share(pieces2.astype(jnp.bfloat16), 2 * col_devs, ("row", "col"), family)
@@ -208,8 +209,7 @@
         gathered.reshape(-1, 2 * col_devs, unit, width), spot, 1, 1, allow_negative_indices=False
     )
     own_unit = own_unit.reshape(pieces2.shape).astype(jnp.float32)
-    answer2 = jnp.where(near, pieces2, own_unit)
-    gathered, kept1, answer2 = lax.optimization_barrier((gathered, kept1, answer2))
+    gathered, kept1, own_unit = lax.optimization_barrier((gathered, kept1, own_unit))
     carried = row_sum(apply_transposed(coupling(offdiag1, kept1), gathered.reshape(-1, width)), 1)
     weighted = (solved1.astype(jnp.float32) - carried).astype(jnp.bfloat16)
     product = apply_transposed(dinv1, flat(share(weighted, col_devs, "col")))
@@ -217,10 +217,11 @@
     slots = jnp.broadcast_to(slots[None], (2,) + slots.shape).reshape(groups[1], -1, unit, width)
     both = total(exchange(slots, "row", own[1]))
     pairs = both.reshape(-1, 2, unit, width)
+    gathered = share(both.astype(jnp.bfloat16), col_devs, "col")
+    pairs, near, pieces2, own_unit = lax.optimization_barrier((pairs, near, pieces2, own_unit))
     answer1 = jnp.where(first, pairs[:, 0], pairs[:, 1])
-    both, answer1 = lax.optimization_barrier((both, answer1))
-
-    gathered, kept0 = lax.optimization_barrier((share(both.astype(jnp.bfloat16), col_devs, "col"), kept0))
+    answer2 = jnp.where(near, pieces2, own_unit)
+    gathered, kept0, answer1, answer2 = lax.optimization_barrier((gathered, kept0, answer1, answer2))
     carried = row_sum(apply_transposed(coupling(offdiag0, kept0), flat(gathered)), 0)
     weighted = (solved0.astype(jnp.float32) - carried).astype(jnp.bfloat16)
     answer0 = row_sum(apply_transposed(again0, flat(share(weighted, col_devs, "col"))), 0)

time: 218 us -> 219 us (level)
  blocking collectives: 179 us -> 169 us
  waiting for transfers between devices: 9.37 us -> 15.6 us
  starting transfers between devices: 11.2 us -> 14.6 us
    all_to_all x17 -> x16, blocking collectives: 179 us -> 169 us  [exchange(): lax.all_to_all(slots, axis, 0, 0, axis_index_groups=groups, tiled=True)]
    all_to_all x2 -> x3, waiting for transfers between devices: 9.36 us -> 15.6 us  [exchange(): lax.all_to_all(slots, axis, 0, 0, axis_index_groups=groups, tiled=True)]
    all_to_all x2 -> x3, starting transfers between devices: 9.31 us -> 12.7 us  [exchange(): lax.all_to_all(slots, axis, 0, 0, axis_index_groups=groups, tiled=True)]
  transfers between devices with their start and end apart: 3 -> 4, of which waited for: 2 -> 3; matrix products, arithmetic and copies ran while one was open for 1% -> 2% of each run, Pallas kernels for 0% -> 0%
where the time goes in v1:
time: 219 us; the launch traced here: 217 us
  blocking collectives  169 us (77%)
  waiting for transfers between devices  15.6 us (7%)
  starting transfers between devices  14.6 us (7%)
  local copies, waits for them, and re-layouts  6.7 us (3%)
  matrix products  4.49 us (2%)
  other arithmetic  3.31 us (2%)
    all_to_all x16, blocking collectives, exchange(): lax.all_to_all(slots, axis, 0, 0, axis_index_groups=groups, tiled=True)  169 us
    all_to_all x3, waiting for transfers between devices, exchange(): lax.all_to_all(slots, axis, 0, 0, axis_index_groups=groups, tiled=True)  15.6 us
    all_to_all x3, starting transfers between devices, exchange(): lax.all_to_all(slots, axis, 0, 0, axis_index_groups=groups, tiled=True)  12.7 us
  transfers between devices with their start and end apart: 4, of which 3 were waited for; matrix products, arithmetic and copies ran while one was open for 2% of the time, Pallas kernels for 0%

profile of v1, /device:TPU:128, one launch (start us, length us, event | category | flops | bytes accessed | tf_op | source)
XLA Modules:
  0.0 217.3 jit_solution(12299144551891851557)
XLA Ops:
  2.2 4.9 %all-to-all-start = ((bf16[4,16,8,128]{3,2,1,0:T(8,128)(2,1)}), bf16[4,16,8,128]{3,2,1,0:T(8,128)(2,1)S(1)}, u32[]{:S(2)}, u32[]{:S(2)}) async-start(bf16[4,16,8,128]{3,2,1,0:T(8,128)(2,1)} %broadcast_in_dim.210), calls=%async_computation | async-start | bytes 262144 | tf_op jit(solution)/shard_map/all_to_all | solution.py:36
  7.1 1.9 collective-permute-start
  11.1 2.1 all-to-all-done
  14.4 2.0 shard_map.121
  16.5 4.4 %all-to-all-start.1 = ((bf16[8,16,8,128]{3,2,1,0:T(8,128)(2,1)}), bf16[8,16,8,128]{3,2,1,0:T(8,128)(2,1)S(1)}, u32[]{:S(2)}, u32[]{:S(2)}) async-start(bf16[8,16,8,128]{3,2,1,0:T(8,128)(2,1)} %bitcast.156), calls=%async_computation.1 | async-start | bytes 524288 | tf_op jit(solution)/shard_map/all_to_all | solution.py:36
  21.1 7.3 %all-to-all-done.1 = bf16[8,16,8,128]{3,2,1,0:T(8,128)(2,1)S(1)} async-done(((bf16[8,16,8,128]{3,2,1,0:T(8,128)(2,1)}), bf16[8,16,8,128]{3,2,1,0:T(8,128)(2,1)S(1)}, u32[]{:S(2)}, u32[]{:S(2)}) %all-to-all-start.1) | async-done | bytes 262176 | tf_op jit(solution)/shard_map/all_to_all | solution.py:36
  28.5 8.9 %all_to_all.95 = bf16[4,16,8,128]{3,2,1,0:T(8,128)(2,1)S(1)} all-to-all(bf16[4,16,8,128]{3,2,1,0:T(8,128)(2,1)S(1)} %broadcast_in_dim.217), channel_id=1, replica_groups={{0,8,16,24},{32,40,48,56},{64,72,80,88},{96,104,112,120},{128,136,144,1..., dimensions={0} | all-to-all | bytes 262144 | tf_op jit(solution)/shard_map/all_to_all | solution.py:36
  38.0 9.9 %all_to_all.96 = bf16[8,16,8,128]{3,2,1,0:T(8,128)(2,1)S(1)} all-to-all(bf16[8,16,8,128]{3,2,1,0:T(8,128)(2,1)S(1)} %bitcast.169), channel_id=1, replica_groups=mesh['row'=64,'col'=8] {'col'}, dimensions={0} | all-to-all | bytes 524288 | tf_op jit(solution)/shard_map/all_to_all | solution.py:36
  48.0 16.8 %all_to_all.97 = bf16[8,8,2,8,128]{4,3,2,1,0:T(8,128)(2,1)S(1)} all-to-all(bf16[8,8,2,8,128]{4,3,2,1,0:T(8,128)(2,1)S(1)} %broadcast_in_dim.220), channel_id=1, replica_groups={{0,8,16,24,32,40,48,56},{64,72,80,88,96,104,112,120},{128,136,144,152,1..., dimensions={0} | all-to-all | bytes 524288 | tf_op jit(solution)/shard_map/all_to_all | solution.py:36
  65.4 8.6 %all_to_all.98 = bf16[8,8,8,128]{3,2,1,0:T(8,128)(2,1)S(1)} all-to-all(bf16[8,8,8,128]{3,2,1,0:T(8,128)(2,1)S(1)} %copy.94), channel_id=1, replica_groups=mesh['row'=64,'col'=8] {'col'}, dimensions={0} | all-to-all | bytes 262144 | tf_op jit(solution)/shard_map/all_to_all | solution.py:36
  74.1 11.5 %all_to_all.99 = bf16[8,8,8,128]{3,2,1,0:T(8,128)(2,1)S(1)} all-to-all(bf16[8,8,8,128]{3,2,1,0:T(8,128)(2,1)S(1)} %broadcast_in_dim.226), channel_id=1, replica_groups={{0,8,16,24,32,40,48,56},{64,72,80,88,96,104,112,120},{128,136,144,152,1..., dimensions={0} | all-to-all | bytes 262144 | tf_op jit(solution)/shard_map/all_to_all | solution.py:36
  86.4 10.8 %all_to_all.100 = bf16[16,4,8,128]{3,2,1,0:T(8,128)(2,1)S(1)} all-to-all(bf16[16,4,8,128]{3,2,1,0:T(8,128)(2,1)S(1)} %bitcast.179), channel_id=1, replica_groups={{0,1,2,3,4,5,6,7,64,65,66,67,68,69,70,71},{8,9,10,11,12,13,14,15,72,73,..., dimensions={0} | all-to-all | bytes 262144 | tf_op jit(solution)/shard_map/all_to_all | solution.py:36
  97.3 11.5 %all_to_all.101 = bf16[16,4,8,128]{3,2,1,0:T(8,128)(2,1)S(1)} all-to-all(bf16[16,4,8,128]{3,2,1,0:T(8,128)(2,1)S(1)} %broadcast_in_dim.229), channel_id=1, replica_groups={{0,8,16,24,32,40,48,56,64,72,80,88,96,104,112,120},{128,136,144,152,160..., dimensions={0} | all-to-all | bytes 262144 | tf_op jit(solution)/shard_map/all_to_all | solution.py:36
  110.2 8.4 %all_to_all.102 = bf16[4,128,128]{2,1,0:T(8,128)(2,1)S(1)} all-to-all(bf16[4,128,128]{2,1,0:T(8,128)(2,1)S(1)} %broadcast_in_dim.230), channel_id=1, replica_groups={{0,2,4,6},{1,3,5,7},{8,10,12,14},{9,11,13,15},{16,18,20,22},{17,19,21,2..., dimensions={0} | all-to-all | bytes 262144 | tf_op jit(solution)/shard_map/all_to_all | solution.py:36
  119.4 11.7 %all_to_all.103 = bf16[16,4,8,128]{3,2,1,0:T(8,128)(2,1)S(1)} all-to-all(bf16[16,4,8,128]{3,2,1,0:T(8,128)(2,1)S(1)} %bitcast.183), channel_id=1, replica_groups={{0,8,16,24,32,40,48,56,64,72,80,88,96,104,112,120},{128,136,144,152,160..., dimensions={0} | all-to-all | bytes 262144 | tf_op jit(solution)/shard_map/all_to_all | solution.py:36
  131.1 9.4 %all_to_all.104 = bf16[16,4,8,128]{3,2,1,0:T(8,128)(2,1)S(1)} all-to-all(bf16[16,4,8,128]{3,2,1,0:T(8,128)(2,1)S(1)} %broadcast_in_dim.231), channel_id=1, replica_groups={{0,1,2,3,4,5,6,7,64,65,66,67,68,69,70,71},{8,9,10,11,12,13,14,15,72,73,..., dimensions={0} | all-to-all | bytes 262144 | tf_op jit(solution)/shard_map/all_to_all | solution.py:36
  141.4 11.8 %all_to_all.105 = bf16[8,8,8,128]{3,2,1,0:T(8,128)(2,1)S(1)} all-to-all(bf16[8,8,8,128]{3,2,1,0:T(8,128)(2,1)S(1)} %bitcast.184), channel_id=1, replica_groups={{0,8,16,24,32,40,48,56},{64,72,80,88,96,104,112,120},{128,136,144,152,1..., dimensions={0} | all-to-all | bytes 262144 | tf_op jit(solution)/shard_map/all_to_all | solution.py:36
  153.3 8.5 %all_to_all.106 = bf16[8,8,8,128]{3,2,1,0:T(8,128)(2,1)S(1)} all-to-all(bf16[8,8,8,128]{3,2,1,0:T(8,128)(2,1)S(1)} %broadcast_in_dim.234), channel_id=1, replica_groups=mesh['row'=64,'col'=8] {'col'}, dimensions={0} | all-to-all | bytes 262144 | tf_op jit(solution)/shard_map/all_to_all | solution.py:36
  162.3 14.4 %all_to_all.107 = bf16[8,16,8,128]{3,2,1,0:T(8,128)(2,1)S(1)} all-to-all(bf16[8,16,8,128]{3,2,1,0:T(8,128)(2,1)S(1)} %bitcast.171), channel_id=1, replica_groups={{0,8,16,24,32,40,48,56},{64,72,80,88,96,104,112,120},{128,136,144,152,1..., dimensions={0} | all-to-all | bytes 524288 | tf_op jit(solution)/shard_map/all_to_all | solution.py:36
  177.5 3.4 %all-to-all-start.15 = ((bf16[8,16,8,128]{3,2,1,0:T(8,128)(2,1)}), bf16[8,16,8,128]{3,2,1,0:T(8,128)(2,1)S(1)}, u32[]{:S(2)}, u32[]{:S(2)}) async-start(bf16[8,16,8,128]{3,2,1,0:T(8,128)(2,1)} %broadcast_in_dim.236), calls=%async_computation.15 | async-start | bytes 524288 | tf_op jit(solution)/shard_map/all_to_all | solution.py:36
  182.1 6.2 %all-to-all-done.15 = bf16[8,16,8,128]{3,2,1,0:T(8,128)(2,1)S(1)} async-done(((bf16[8,16,8,128]{3,2,1,0:T(8,128)(2,1)}), bf16[8,16,8,128]{3,2,1,0:T(8,128)(2,1)S(1)}, u32[]{:S(2)}, u32[]{:S(2)}) %all-to-all-start.15) | async-done | bytes 262176 | tf_op jit(solution)/shard_map/all_to_all | solution.py:36
  189.0 8.6 %all_to_all.108 = bf16[4,16,8,128]{3,2,1,0:T(8,128)(2,1)S(1)} all-to-all(bf16[4,16,8,128]{3,2,1,0:T(8,128)(2,1)S(1)} %bitcast.186), channel_id=1, replica_groups={{0,8,16,24},{32,40,48,56},{64,72,80,88},{96,104,112,120},{128,136,144,1..., dimensions={0} | all-to-all | bytes 262144 | tf_op jit(solution)/shard_map/all_to_all | solution.py:36
  197.7 9.9 %all_to_all.109 = bf16[8,16,8,128]{3,2,1,0:T(8,128)(2,1)S(1)} all-to-all(bf16[8,16,8,128]{3,2,1,0:T(8,128)(2,1)S(1)} %broadcast_in_dim.240), channel_id=1, replica_groups=mesh['row'=64,'col'=8] {'col'}, dimensions={0} | all-to-all | bytes 524288 | tf_op jit(solution)/shard_map/all_to_all | solution.py:36
  208.2 8.5 %all_to_all.110 = bf16[4,16,8,128]{3,2,1,0:T(8,128)(2,1)S(1)} all-to-all(bf16[4,16,8,128]{3,2,1,0:T(8,128)(2,1)S(1)} %bitcast.187), channel_id=1, replica_groups={{0,8,16,24},{32,40,48,56},{64,72,80,88},{96,104,112,120},{128,136,144,1..., dimensions={0} | all-to-all | bytes 262144 | tf_op jit(solution)/shard_map/all_to_all | solution.py:36
  (117 shorter events, 14.5 us)
Async XLA Ops:
  0.6 64.3 %copy-start = (bf16[512,512]{1,0:T(8,128)(2,1)S(1)}, bf16[512,512]{1,0:T(8,128)(2,1)}, u32[]{:S(2)}) copy-start(bf16[512,512]{1,0:T(8,128)(2,1)} %param.11) | copy-start | bytes 1572868
  0.6 12.5 %copy-start.1 = (bf16[1024,512]{1,0:T(8,128)(2,1)S(1)}, bf16[1024,512]{1,0:T(8,128)(2,1)}, u32[]{:S(2)}) copy-start(bf16[1024,512]{1,0:T(8,128)(2,1)} %source_ref) | copy-start | bytes 3145732
  2.2 10.9 %all-to-all-start = ((bf16[4,16,8,128]{3,2,1,0:T(8,128)(2,1)}), bf16[4,16,8,128]{3,2,1,0:T(8,128)(2,1)S(1)}, u32[]{:S(2)}, u32[]{:S(2)}) async-start(bf16[4,16,8,128]{3,2,1,0:T(8,128)(2,1)} %broadcast_in_dim.210), calls=%async_computation | async-start | bytes 262144 | tf_op jit(solution)/shard_map/all_to_all | solution.py:36
  7.1 6.1 %collective-permute-start = (bf16[256,512]{1,0:T(8,128)(2,1)}, bf16[256,512]{1,0:T(8,128)(2,1)S(1)}, u32[]{:S(2)}, u32[]{:S(2)}) collective-permute-start(bf16[256,512]{1,0:T(8,128)(2,1)} %param.12), channel_id=1, source_target_pairs={{0,1},{1,0},{2,3},{3,2},{4,5},{5,4},{6,7},{7,6},{8,9},{9,8},{10,11... | collective-permute-start | bytes 786440 | tf_op jit(solution)/shard_map/ppermute | solution.py:148
  14.4 6.6 %copy-start.7 = (bf16[32,128]{1,0:T(8,128)(2,1)S(1)}, bf16[32,128]{1,0:T(8,128)(2,1)}, u32[]{:S(2)}) copy-start(bf16[32,128]{1,0:T(8,128)(2,1)} %param.17) | copy-start | bytes 24580
  14.4 6.6 %copy-start.6 = (bf16[64,128]{1,0:T(8,128)(2,1)S(1)}, bf16[64,128]{1,0:T(8,128)(2,1)}, u32[]{:S(2)}) copy-start(bf16[64,128]{1,0:T(8,128)(2,1)} %param.16) | copy-start | bytes 49156
  16.4 21.0 %copy-start.2 = (bf16[1024,512]{1,0:T(8,128)(2,1)S(1)}, bf16[1024,512]{1,0:T(8,128)(2,1)}, u32[]{:S(2)}) copy-start(bf16[1024,512]{1,0:T(8,128)(2,1)} %param.13) | copy-start | bytes 3145732
  16.5 11.9 %all-to-all-start.1 = ((bf16[8,16,8,128]{3,2,1,0:T(8,128)(2,1)}), bf16[8,16,8,128]{3,2,1,0:T(8,128)(2,1)S(1)}, u32[]{:S(2)}, u32[]{:S(2)}) async-start(bf16[8,16,8,128]{3,2,1,0:T(8,128)(2,1)} %bitcast.156), calls=%async_computation.1 | async-start | bytes 524288 | tf_op jit(solution)/shard_map/all_to_all | solution.py:36
  65.4 20.3 %copy-start.4 = (bf16[512,512]{1,0:T(8,128)(2,1)S(1)}, bf16[512,512]{1,0:T(8,128)(2,1)}, u32[]{:S(2)}) copy-start(bf16[512,512]{1,0:T(8,128)(2,1)} %param.14) | copy-start | bytes 1572868
  108.9 1.0 copy-start.5
  177.5 10.8 %all-to-all-start.15 = ((bf16[8,16,8,128]{3,2,1,0:T(8,128)(2,1)}), bf16[8,16,8,128]{3,2,1,0:T(8,128)(2,1)S(1)}, u32[]{:S(2)}, u32[]{:S(2)}) async-start(bf16[8,16,8,128]{3,2,1,0:T(8,128)(2,1)} %broadcast_in_dim.236), calls=%async_computation.15 | async-start | bytes 524288 | tf_op jit(solution)/shard_map/all_to_all | solution.py:36
  189.0 18.7 %copy-start.3 = (bf16[1024,512]{1,0:T(8,128)(2,1)S(1)}, bf16[1024,512]{1,0:T(8,128)(2,1)}, u32[]{:S(2)}) copy-start(bf16[1024,512]{1,0:T(8,128)(2,1)} %shard_map.121) | copy-start | bytes 3145732

commit v2 on v0

--- a/solution.py
+++ b/solution.py
@@ -138,27 +138,28 @@
         slots = product.reshape(-1, groups[level], unit, width).transpose(1, 0, 2, 3)
         return total(exchange(slots, "row", own[level]))
 
-    gathered, kept0, kept1, inverse0, other2 = lax.optimization_barrier(
+    gathered, kept0, inverse0, other2 = lax.optimization_barrier(
         (
             row_gather(rhs0.reshape(-1, unit, width), 0),
             kept(offdiag0, block_rows0, groups[0]),
-            kept(offdiag1, block_rows1, groups[1]),
             dinv0,
             lax.ppermute(dinv2, "col", [(i, i ^ 1) for i in range(col_devs)]),
         )
     )
-    slots, late1, late2, half, upper, column = lax.optimization_barrier(
-        (column_slots(apply_plain(inverse0, flat(gathered))), rhs1, rhs2, half, upper, column)
+    slots, listing1, late1, late2, half, upper, column = lax.optimization_barrier(
+        (column_slots(apply_plain(inverse0, flat(gathered))), block_rows1, rhs1, rhs2, half, upper, column)
     )
     received = exchange(slots, "col")
     again0 = second_copy(inverse0)
+    kept1 = kept(offdiag1, listing1, groups[1])
     mine = lax.broadcasted_iota(jnp.int32, (1, 2, 1, 1), 1) == half
     destination = lax.broadcasted_iota(jnp.int32, (1, 2 * col_devs, 1, 1), 1)
     here = destination == upper * col_devs + column
-    received, again0, side1, side2, first, near, low, spot = lax.optimization_barrier(
+    received, again0, kept1, side1, side2, first, near, low, spot = lax.optimization_barrier(
         (
             received,
             again0,
+            kept1,
             jnp.where(mine, late1.reshape(-1, 1, unit, width).astype(jnp.float32), 0.0),
             jnp.where(here, late2.reshape(-1, 1, unit, width).astype(jnp.float32), 0.0),
             half == 0,

time: 218 us -> 219 us (level)
  no operation moved by 1% of the time
where the time goes in v2:
time: 219 us; the launch traced here: 218 us
  blocking collectives  179 us (82%)
  starting transfers between devices  11.2 us (5%)
  waiting for transfers between devices  10.3 us (5%)
  local copies, waits for them, and re-layouts  5.58 us (3%)
  matrix products  5.39 us (2%)
  other arithmetic  3.38 us (2%)
    all_to_all x17, blocking collectives, exchange(): lax.all_to_all(slots, axis, 0, 0, axis_index_groups=groups, tiled=True)  179 us
    all_to_all x2, waiting for transfers between devices, exchange(): lax.all_to_all(slots, axis, 0, 0, axis_index_groups=groups, tiled=True)  10.3 us
    all_to_all x2, starting transfers between devices, exchange(): lax.all_to_all(slots, axis, 0, 0, axis_index_groups=groups, tiled=True)  9.31 us
  transfers between devices with their start and end apart: 3, of which 2 were waited for; matrix products, arithmetic and copies ran while one was open for 1% of the time, Pallas kernels for 0%

profile of v2, /device:TPU:128, one launch (start us, length us, event | category | flops | bytes accessed | tf_op | source)
XLA Modules:
  0.0 218.3 jit_solution(6874751308609172862)
XLA Ops:
  2.1 4.9 %all-to-all-start = ((bf16[4,16,8,128]{3,2,1,0:T(8,128)(2,1)}), bf16[4,16,8,128]{3,2,1,0:T(8,128)(2,1)S(1)}, u32[]{:S(2)}, u32[]{:S(2)}) async-start(bf16[4,16,8,128]{3,2,1,0:T(8,128)(2,1)} %broadcast_in_dim.210), calls=%async_computation | async-start | bytes 262144 | tf_op jit(solution)/shard_map/all_to_all | solution.py:36
  7.0 1.9 collective-permute-start
  10.1 3.0 %all-to-all-done = bf16[4,16,8,128]{3,2,1,0:T(8,128)(2,1)S(1)} async-done(((bf16[4,16,8,128]{3,2,1,0:T(8,128)(2,1)}), bf16[4,16,8,128]{3,2,1,0:T(8,128)(2,1)S(1)}, u32[]{:S(2)}, u32[]{:S(2)}) %all-to-all-start) | async-done | bytes 131104 | tf_op jit(solution)/shard_map/all_to_all | solution.py:36
  13.1 1.7 convolution_convert_fusion.1
  15.6 2.0 shard_map.121
  18.6 4.4 %all-to-all-start.1 = ((bf16[8,16,8,128]{3,2,1,0:T(8,128)(2,1)}), bf16[8,16,8,128]{3,2,1,0:T(8,128)(2,1)S(1)}, u32[]{:S(2)}, u32[]{:S(2)}) async-start(bf16[8,16,8,128]{3,2,1,0:T(8,128)(2,1)} %bitcast.160), calls=%async_computation.1 | async-start | bytes 524288 | tf_op jit(solution)/shard_map/all_to_all | solution.py:36
  23.2 7.3 %all-to-all-done.1 = bf16[8,16,8,128]{3,2,1,0:T(8,128)(2,1)S(1)} async-done(((bf16[8,16,8,128]{3,2,1,0:T(8,128)(2,1)}), bf16[8,16,8,128]{3,2,1,0:T(8,128)(2,1)S(1)}, u32[]{:S(2)}, u32[]{:S(2)}) %all-to-all-start.1) | async-done | bytes 262176 | tf_op jit(solution)/shard_map/all_to_all | solution.py:36
  30.6 8.6 %all_to_all.95 = bf16[4,16,8,128]{3,2,1,0:T(8,128)(2,1)S(1)} all-to-all(bf16[4,16,8,128]{3,2,1,0:T(8,128)(2,1)S(1)} %broadcast_in_dim.217), channel_id=1, replica_groups={{0,8,16,24},{32,40,48,56},{64,72,80,88},{96,104,112,120},{128,136,144,1..., dimensions={0} | all-to-all | bytes 262144 | tf_op jit(solution)/shard_map/all_to_all | solution.py:36
  39.8 9.9 %all_to_all.96 = bf16[8,16,8,128]{3,2,1,0:T(8,128)(2,1)S(1)} all-to-all(bf16[8,16,8,128]{3,2,1,0:T(8,128)(2,1)S(1)} %bitcast.169), channel_id=1, replica_groups=mesh['row'=64,'col'=8] {'col'}, dimensions={0} | all-to-all | bytes 524288 | tf_op jit(solution)/shard_map/all_to_all | solution.py:36
  49.8 17.0 %all_to_all.97 = bf16[8,8,2,8,128]{4,3,2,1,0:T(8,128)(2,1)S(1)} all-to-all(bf16[8,8,2,8,128]{4,3,2,1,0:T(8,128)(2,1)S(1)} %broadcast_in_dim.220), channel_id=1, replica_groups={{0,8,16,24,32,40,48,56},{64,72,80,88,96,104,112,120},{128,136,144,152,1..., dimensions={0} | all-to-all | bytes 524288 | tf_op jit(solution)/shard_map/all_to_all | solution.py:36
  67.4 8.6 %all_to_all.98 = bf16[8,8,8,128]{3,2,1,0:T(8,128)(2,1)S(1)} all-to-all(bf16[8,8,8,128]{3,2,1,0:T(8,128)(2,1)S(1)} %copy.129), channel_id=1, replica_groups=mesh['row'=64,'col'=8] {'col'}, dimensions={0} | all-to-all | bytes 262144 | tf_op jit(solution)/shard_map/all_to_all | solution.py:36
  76.0 11.5 %all_to_all.99 = bf16[8,8,8,128]{3,2,1,0:T(8,128)(2,1)S(1)} all-to-all(bf16[8,8,8,128]{3,2,1,0:T(8,128)(2,1)S(1)} %broadcast_in_dim.226), channel_id=1, replica_groups={{0,8,16,24,32,40,48,56},{64,72,80,88,96,104,112,120},{128,136,144,152,1..., dimensions={0} | all-to-all | bytes 262144 | tf_op jit(solution)/shard_map/all_to_all | solution.py:36
  88.4 10.8 %all_to_all.100 = bf16[16,4,8,128]{3,2,1,0:T(8,128)(2,1)S(1)} all-to-all(bf16[16,4,8,128]{3,2,1,0:T(8,128)(2,1)S(1)} %bitcast.179), channel_id=1, replica_groups={{0,1,2,3,4,5,6,7,64,65,66,67,68,69,70,71},{8,9,10,11,12,13,14,15,72,73,..., dimensions={0} | all-to-all | bytes 262144 | tf_op jit(solution)/shard_map/all_to_all | solution.py:36
  99.3 11.5 %all_to_all.101 = bf16[16,4,8,128]{3,2,1,0:T(8,128)(2,1)S(1)} all-to-all(bf16[16,4,8,128]{3,2,1,0:T(8,128)(2,1)S(1)} %broadcast_in_dim.229), channel_id=1, replica_groups={{0,8,16,24,32,40,48,56,64,72,80,88,96,104,112,120},{128,136,144,152,160..., dimensions={0} | all-to-all | bytes 262144 | tf_op jit(solution)/shard_map/all_to_all | solution.py:36
  111.6 8.4 %all_to_all.102 = bf16[4,128,128]{2,1,0:T(8,128)(2,1)S(1)} all-to-all(bf16[4,128,128]{2,1,0:T(8,128)(2,1)S(1)} %broadcast_in_dim.230), channel_id=1, replica_groups={{0,2,4,6},{1,3,5,7},{8,10,12,14},{9,11,13,15},{16,18,20,22},{17,19,21,2..., dimensions={0} | all-to-all | bytes 262144 | tf_op jit(solution)/shard_map/all_to_all | solution.py:36
  120.8 11.7 %all_to_all.103 = bf16[16,4,8,128]{3,2,1,0:T(8,128)(2,1)S(1)} all-to-all(bf16[16,4,8,128]{3,2,1,0:T(8,128)(2,1)S(1)} %copy.147), channel_id=1, replica_groups={{0,8,16,24,32,40,48,56,64,72,80,88,96,104,112,120},{128,136,144,152,160..., dimensions={0} | all-to-all | bytes 262144 | tf_op jit(solution)/shard_map/all_to_all | solution.py:36
  132.5 9.4 %all_to_all.104 = bf16[16,4,8,128]{3,2,1,0:T(8,128)(2,1)S(1)} all-to-all(bf16[16,4,8,128]{3,2,1,0:T(8,128)(2,1)S(1)} %broadcast_in_dim.231), channel_id=1, replica_groups={{0,1,2,3,4,5,6,7,64,65,66,67,68,69,70,71},{8,9,10,11,12,13,14,15,72,73,..., dimensions={0} | all-to-all | bytes 262144 | tf_op jit(solution)/shard_map/all_to_all | solution.py:36
  143.4 11.8 %all_to_all.105 = bf16[8,8,8,128]{3,2,1,0:T(8,128)(2,1)S(1)} all-to-all(bf16[8,8,8,128]{3,2,1,0:T(8,128)(2,1)S(1)} %bitcast.184), channel_id=1, replica_groups={{0,8,16,24,32,40,48,56},{64,72,80,88,96,104,112,120},{128,136,144,152,1..., dimensions={0} | all-to-all | bytes 262144 | tf_op jit(solution)/shard_map/all_to_all | solution.py:36
  155.3 8.5 %all_to_all.106 = bf16[8,8,8,128]{3,2,1,0:T(8,128)(2,1)S(1)} all-to-all(bf16[8,8,8,128]{3,2,1,0:T(8,128)(2,1)S(1)} %broadcast_in_dim.235), channel_id=1, replica_groups=mesh['row'=64,'col'=8] {'col'}, dimensions={0} | all-to-all | bytes 262144 | tf_op jit(solution)/shard_map/all_to_all | solution.py:36
  164.3 14.4 %all_to_all.107 = bf16[8,16,8,128]{3,2,1,0:T(8,128)(2,1)S(1)} all-to-all(bf16[8,16,8,128]{3,2,1,0:T(8,128)(2,1)S(1)} %bitcast.171), channel_id=1, replica_groups={{0,8,16,24,32,40,48,56},{64,72,80,88,96,104,112,120},{128,136,144,152,1..., dimensions={0} | all-to-all | bytes 524288 | tf_op jit(solution)/shard_map/all_to_all | solution.py:36
  179.3 9.9 %all_to_all.108 = bf16[8,16,8,128]{3,2,1,0:T(8,128)(2,1)S(1)} all-to-all(bf16[8,16,8,128]{3,2,1,0:T(8,128)(2,1)S(1)} %broadcast_in_dim.237), channel_id=1, replica_groups=mesh['row'=64,'col'=8] {'col'}, dimensions={0} | all-to-all | bytes 524288 | tf_op jit(solution)/shard_map/all_to_all | solution.py:36
  189.9 8.6 %all_to_all.109 = bf16[4,16,8,128]{3,2,1,0:T(8,128)(2,1)S(1)} all-to-all(bf16[4,16,8,128]{3,2,1,0:T(8,128)(2,1)S(1)} %bitcast.186), channel_id=1, replica_groups={{0,8,16,24},{32,40,48,56},{64,72,80,88},{96,104,112,120},{128,136,144,1..., dimensions={0} | all-to-all | bytes 262144 | tf_op jit(solution)/shard_map/all_to_all | solution.py:36
  198.6 9.9 %all_to_all.110 = bf16[8,16,8,128]{3,2,1,0:T(8,128)(2,1)S(1)} all-to-all(bf16[8,16,8,128]{3,2,1,0:T(8,128)(2,1)S(1)} %broadcast_in_dim.240), channel_id=1, replica_groups=mesh['row'=64,'col'=8] {'col'}, dimensions={0} | all-to-all | bytes 524288 | tf_op jit(solution)/shard_map/all_to_all | solution.py:36
  209.1 8.5 %all_to_all.111 = bf16[4,16,8,128]{3,2,1,0:T(8,128)(2,1)S(1)} all-to-all(bf16[4,16,8,128]{3,2,1,0:T(8,128)(2,1)S(1)} %bitcast.187), channel_id=1, replica_groups={{0,8,16,24},{32,40,48,56},{64,72,80,88},{96,104,112,120},{128,136,144,1..., dimensions={0} | all-to-all | bytes 262144 | tf_op jit(solution)/shard_map/all_to_all | solution.py:36
  (117 shorter events, 12.7 us)
Async XLA Ops:
  0.6 66.2 %copy-start = (bf16[512,512]{1,0:T(8,128)(2,1)S(1)}, bf16[512,512]{1,0:T(8,128)(2,1)}, u32[]{:S(2)}) copy-start(bf16[512,512]{1,0:T(8,128)(2,1)} %param.11) | copy-start | bytes 1572868
  0.6 6.4 %copy-start.4 = (bf16[256,512]{1,0:T(8,128)(2,1)S(1)}, bf16[256,512]{1,0:T(8,128)(2,1)}, u32[]{:S(2)}) copy-start(bf16[256,512]{1,0:T(8,128)(2,1)} %param.12) | copy-start | bytes 786436
  2.1 10.9 %all-to-all-start = ((bf16[4,16,8,128]{3,2,1,0:T(8,128)(2,1)}), bf16[4,16,8,128]{3,2,1,0:T(8,128)(2,1)S(1)}, u32[]{:S(2)}, u32[]{:S(2)}) async-start(bf16[4,16,8,128]{3,2,1,0:T(8,128)(2,1)} %broadcast_in_dim.210), calls=%async_computation | async-start | bytes 262144 | tf_op jit(solution)/shard_map/all_to_all | solution.py:36
  7.0 6.1 %collective-permute-start = (bf16[256,512]{1,0:T(8,128)(2,1)S(1)}, bf16[256,512]{1,0:T(8,128)(2,1)S(1)}, u32[]{:S(2)}, u32[]{:S(2)}) collective-permute-start(bf16[256,512]{1,0:T(8,128)(2,1)S(1)} %copy-done.4), channel_id=1, source_target_pairs={{0,1},{1,0},{2,3},{3,2},{4,5},{5,4},{6,7},{7,6},{8,9},{9,8},{10,11... | collective-permute-start | bytes 786440 | tf_op jit(solution)/shard_map/ppermute | solution.py:146
  15.5 7.5 %copy-start.6 = (bf16[32,128]{1,0:T(8,128)(2,1)S(1)}, bf16[32,128]{1,0:T(8,128)(2,1)}, u32[]{:S(2)}) copy-start(bf16[32,128]{1,0:T(8,128)(2,1)} %param.17) | copy-start | bytes 24580
  15.5 7.5 %copy-start.5 = (bf16[64,128]{1,0:T(8,128)(2,1)S(1)}, bf16[64,128]{1,0:T(8,128)(2,1)}, u32[]{:S(2)}) copy-start(bf16[64,128]{1,0:T(8,128)(2,1)} %param.16) | copy-start | bytes 49156
  18.3 20.9 %copy-start.1 = (bf16[1024,512]{1,0:T(8,128)(2,1)S(1)}, bf16[1024,512]{1,0:T(8,128)(2,1)}, u32[]{:S(2)}) copy-start(bf16[1024,512]{1,0:T(8,128)(2,1)} %param.13) | copy-start | bytes 3145732
  18.6 12.0 %all-to-all-start.1 = ((bf16[8,16,8,128]{3,2,1,0:T(8,128)(2,1)}), bf16[8,16,8,128]{3,2,1,0:T(8,128)(2,1)S(1)}, u32[]{:S(2)}, u32[]{:S(2)}) async-start(bf16[8,16,8,128]{3,2,1,0:T(8,128)(2,1)} %bitcast.160), calls=%async_computation.1 | async-start | bytes 524288 | tf_op jit(solution)/shard_map/all_to_all | solution.py:36
  67.4 20.3 %copy-start.3 = (bf16[512,512]{1,0:T(8,128)(2,1)S(1)}, bf16[512,512]{1,0:T(8,128)(2,1)}, u32[]{:S(2)}) copy-start(bf16[512,512]{1,0:T(8,128)(2,1)} %param.14) | copy-start | bytes 1572868
  189.9 18.7 %copy-start.2 = (bf16[1024,512]{1,0:T(8,128)(2,1)S(1)}, bf16[1024,512]{1,0:T(8,128)(2,1)}, u32[]{:S(2)}) copy-start(bf16[1024,512]{1,0:T(8,128)(2,1)} %shard_map.121) | copy-start | bytes 3145732
